TPU v7x, 32 devices: a whole 2x2x4 slice. The times are simulated.
32 devices in a mesh: seq: 8 (over z, y), chan: 2 (over x), section: 2 (over core).
Axes of the slice: x: 2, y: 2, z: 4, core: 2. Of those that a mesh axis runs over, the one named last changes fastest.
Arguments:
- tokens: bfloat16 [2, 2048, 1024], P(None, 'seq', 'chan'), may hold values from -6 to 6
- in_proj: bfloat16 [2, 1024, 2, 1024], P('section', None, None, 'chan'), may hold values from -0.1875 to 0.1875
- filters: bfloat16 [2, 8, 2304], P('section', 'chan'), may hold values from -0.13183594 to 0.13183594
- out_proj: bfloat16 [2, 1024, 1024], P('section', None, 'chan'), may hold values from -0.1875 to 0.1875
- widths: int32 [2], replicated, may hold values from 1 to 4, as said below
Outputs:
- layer_outputs: bfloat16 [2, 2, 2048, 1024], P('section', None, 'seq', 'chan')
Inputs may be any that keep to these rules, and one draw needn't show every extreme that they name: `widths`: exactly one sequence has width 8 / 2.
All inputs are finite; a program needn't handle non-finite values.
Results may differ from a plain program's by a relative error of at most 0.0077.
Values may be sent and summed in bfloat16 or wider, within the bound.
No kernel may reach another device: no remote copies, remote signals or barrier semaphores. Data moves between devices by JAX's collectives and lax.ppermute only.
A program may use at most 64 MiB of HBM per device.

v0:
```python
import jax
import jax.numpy as jnp
from jax import lax
from jax.sharding import PartitionSpec as P

BLK = 256
BAND = 8
MB = 2


def shifted(value, axis, by):
    size = lax.axis_size(axis)
    return lax.ppermute(value, axis, [(i, (i + by) % size) for i in range(size)])


def shifted_2(value, axis, steps):
    count = lax.axis_size(axis)
    leading, last = (max(0, -steps), min(count, count - steps))
    return lax.ppermute(value, axis, [(source, source + steps) for source in range(leading, last)])


def lookup(table, row_index):
    return jnp.sum(jnp.where(jnp.arange(table.shape[0]) == row_index, table, 0))


def toeplitz_stack(taps):
    reach = BAND // 2
    windows = jnp.stack(
        [
            taps[:, BLK * (block_lag + reach + 1) - BLK + 1 : BLK * (block_lag + reach + 1) + BLK]
            for block_lag in range(-reach, reach)
        ]
    )
    reverse = windows[..., ::-1]
    padded = jnp.pad(reverse, ((0, 0), (0, 0), (0, 1)))
    tiled = jnp.tile(padded, (1, 1, BLK))
    shaped = tiled[..., : BLK * (2 * BLK - 1)].reshape(BAND, taps.shape[0], BLK, 2 * BLK - 1)
    return shaped[..., BLK - 1 :]


def convolve(signal, toeplitz, widths, micro_batch):
    reach = BAND // 2
    block_len, local_width = signal.shape
    local_heads = toeplitz.shape[1]
    head_width = local_width // local_heads
    band_width = lookup(widths, micro_batch)

    def in_band(block_lag):
        return ((block_lag >= -band_width) & (block_lag < band_width)).astype(jnp.float32)

    def toeplitz_apply(block_lag, source):
        shaped = source.reshape(block_len, local_heads, head_width)
        product = jnp.einsum(
            "hts,shc->thc", toeplitz[block_lag + reach], shaped, preferred_element_type=jnp.float32
        )
        return product.reshape(block_len, local_width)

    summed = in_band(0) * toeplitz_apply(0, signal)
    for block_lag in range(-reach, reach):
        if block_lag != 0:
            fetched = shifted(signal, "seq", block_lag)
            summed = summed + in_band(block_lag) * toeplitz_apply(block_lag, fetched)
    return summed


def per_device(tokens, in_proj, filters, out_proj, widths):
    section_index = lax.axis_index("section")
    section_count = lax.axis_size("section")
    block_len, local_width = (tokens.shape[1], tokens.shape[2])
    toeplitz = toeplitz_stack(filters[0])
    input_weight = in_proj[0]
    output_weight = out_proj[0]
    received = jnp.zeros((block_len, local_width), jnp.bfloat16)
    record = jnp.zeros((1, MB, block_len, local_width), jnp.bfloat16)
    step_count = MB + section_count - 1
    for step_index in range(step_count):
        own_input = tokens[min(step_index, MB - 1)]
        layer_input = jnp.where(section_index == 0, own_input, received)
        projected = jnp.einsum(
            "tk,kjc->tjc",
            lax.all_gather(layer_input, "chan", axis=1, tiled=True),
            input_weight,
            preferred_element_type=jnp.float32,
        )
        signal = projected[:, 0, :].astype(jnp.bfloat16)
        gating = projected[:, 1, :].astype(jnp.bfloat16)
        micro_batch = jnp.clip(step_index - section_index, 0, MB - 1)
        mixed = convolve(signal, toeplitz, widths, micro_batch)
        gated = (jax.nn.silu(gating.astype(jnp.float32)) * mixed).astype(jnp.bfloat16)
        result = jnp.dot(
            lax.all_gather(gated, "chan", axis=1, tiled=True),
            output_weight,
            preferred_element_type=jnp.float32,
        ).astype(jnp.bfloat16)
        slot_mask = jnp.arange(MB) == step_index - section_index
        record = jnp.where(slot_mask[None, :, None, None], result[None, None], record)
        if step_index + 1 < step_count:
            received = shifted_2(result, "section", 1)
    return record


def solution(mesh):
    placed = (
        P(None, "seq", "chan"),
        P("section", None, None, "chan"),
        P("section", "chan", None),
        P("section", None, "chan"),
        P(),
    )
    return jax.shard_map(
        per_device,
        mesh=mesh,
        in_specs=placed,
        out_specs=P("section", None, "seq", "chan"),
        check_vma=False,
    )
```

profile of v0, /device:TPU:14, one launch (start us, length us, event | category | flops | bytes accessed | tf_op | source)
XLA Modules:
  0.0 278.9 jit_solution(6058741622228252631)
XLA Ops:
  1.1 8.7 %all-gather = bf16[1,256,1024]{2,1,0:T(8,128)(2,1)S(1)} all-gather(bf16[1,256,512]{2,1,0:T(8,128)(2,1)S(1)} %slice_select_fusion), channel_id=2, replica_groups=mesh['seq'=8,'chan'=2,'section'=2] {'chan'}, dimensions={2}, use_global_device_ids=true | all-gather | bytes 786432 | tf_op jit(solution)/shard_map/all_gather | solution.py:81
  11.3 2.6 collective-permute-start
  31.9 3.8 %tile.4 = bf16[8,4,256,512]{3,0,2,1:T(8,128)(2,1)} broadcast(bf16[8,4,512]{2,0,1:T(8,128)(2,1)S(1)} %pad.4.clone), dimensions={0,1,3} | broadcast | bytes 8421376 | tf_op jit(solution)/shard_map/tile | solution.py:36
  35.7 7.1 %slice.139 = bf16[8,4,130816]{2,0,1:T(8,128)(2,1)} slice(bf16[8,4,131072]{2,0,1:T(8,128)(2,1)} %bitcast.198), slice={[0:8], [0:4], [0:130816]} | slice | bytes 16744448 | tf_op jit(solution)/shard_map/slice | solution.py:37
  42.9 19.5 %reshape.214 = bf16[8,4,256,511]{3,2,0,1:T(8,128)(2,1)} reshape(bf16[8,4,130816]{2,0,1:T(8,128)(2,1)} %slice.139) | data formatting | bytes 16744448 | tf_op jit(solution)/shard_map/reshape | solution.py:37
  66.9 2.4 fusion.26
  72.6 2.4 convolution_multiply_fusion.17
  89.9 3.3 %fusion.25 = f32[4,128,256]{2,1,0:T(8,128)} fusion(f32[4,128,256]{2,1,0:T(8,128)} %convolution_multiply_fusion.16, f32[4,128,256]{2,1,0:T(8,128)} %convolution_multiply_fusion.17, f32[4,128,256]{2,1,0:T(8,128)} %convolution_multiply_fusion.18, f32[4,128,256]{2,1,0:T(8,128)} %convolution_multiply_fusion.19, f32[4,128,256]{2,1,0:T(8,128)} %convolution_multiply_fusion.20, ...), kind=kOutput, calls=%fused_computation.47 | convolution fusion | flops 68026368 | bytes 4456452 | tf_op jit(solution)/shard_map/hts,shc->thc/dot_general | solution.py:53
  96.6 7.0 %all_gather.19 = bf16[256,1024]{1,0:T(8,128)(2,1)S(1)} all-gather(bf16[256,512]{1,0:T(8,128)(2,1)S(1)} %fusion.47), channel_id=1, replica_groups=mesh['seq'=8,'chan'=2,'section'=2] {'chan'}, dimensions={1}, use_global_device_ids=true | all-gather | bytes 786432 | tf_op jit(solution)/shard_map/all_gather | solution.py:91
  107.5 9.2 %all_gather.20 = bf16[256,1024]{1,0:T(8,128)(2,1)S(1)} all-gather(bf16[256,512]{1,0:T(8,128)(2,1)S(1)} %bitcast_select_fusion.1), channel_id=1, replica_groups=mesh['seq'=8,'chan'=2,'section'=2] {'chan'}, dimensions={1}, use_global_device_ids=true | all-gather | bytes 786432 | tf_op jit(solution)/shard_map/all_gather | solution.py:81
  119.1 2.5 collective-permute-start.8
  139.6 7.8 %collective-permute-start.14 = (bf16[256,512]{1,0:T(8,128)(2,1)}, bf16[256,512]{1,0:T(8,128)(2,1)}, u32[]{:S(2)}, u32[]{:S(2)}) collective-permute-start(bf16[256,512]{1,0:T(8,128)(2,1)} %slice_bitcast_fusion.41), channel_id=1, source_target_pairs={{0,12},{4,16},{8,20},{12,24},{16,28},{20,0},{24,4},{28,8},{1,13},{... | collective-permute-start | bytes 786440 | tf_op jit(solution)/shard_map/ppermute | solution.py:13
  148.4 2.5 fusion.19
  150.9 4.2 %collective-permute-done.10 = bf16[256,512]{1,0:T(8,128)(2,1)} collective-permute-done((bf16[256,512]{1,0:T(8,128)(2,1)}, bf16[256,512]{1,0:T(8,128)(2,1)}, u32[]{:S(2)}, u32[]{:S(2)}) %collective-permute-start.10) | collective-permute-done | bytes 262176 | tf_op jit(solution)/shard_map/ppermute | solution.py:13
  158.6 6.9 %collective-permute-done.11 = bf16[256,512]{1,0:T(8,128)(2,1)} collective-permute-done((bf16[256,512]{1,0:T(8,128)(2,1)}, bf16[256,512]{1,0:T(8,128)(2,1)}, u32[]{:S(2)}, u32[]{:S(2)}) %collective-permute-start.11) | collective-permute-done | bytes 262176 | tf_op jit(solution)/shard_map/ppermute | solution.py:13
  180.3 3.3 %fusion.18 = f32[4,128,256]{2,1,0:T(8,128)} fusion(f32[4,128,256]{2,1,0:T(8,128)} %convolution_multiply_fusion.8, f32[4,128,256]{2,1,0:T(8,128)} %convolution_multiply_fusion.9, f32[4,128,256]{2,1,0:T(8,128)} %convolution_multiply_fusion.10, f32[4,128,256]{2,1,0:T(8,128)} %convolution_multiply_fusion.11, f32[4,128,256]{2,1,0:T(8,128)} %convolution_multiply_fusion.12, ...), kind=kOutput, calls=%fused_computation.32 | convolution fusion | flops 68026368 | bytes 4456452 | tf_op jit(solution)/shard_map/hts,shc->thc/dot_general | solution.py:53
  186.9 7.0 %all_gather.21 = bf16[256,1024]{1,0:T(8,128)(2,1)S(1)} all-gather(bf16[256,512]{1,0:T(8,128)(2,1)S(1)} %fusion.46), channel_id=1, replica_groups=mesh['seq'=8,'chan'=2,'section'=2] {'chan'}, dimensions={1}, use_global_device_ids=true | all-gather | bytes 786432 | tf_op jit(solution)/shard_map/all_gather | solution.py:91
  197.8 9.2 %all_gather.22 = bf16[256,1024]{1,0:T(8,128)(2,1)S(1)} all-gather(bf16[256,512]{1,0:T(8,128)(2,1)S(1)} %bitcast_select_fusion), channel_id=1, replica_groups=mesh['seq'=8,'chan'=2,'section'=2] {'chan'}, dimensions={1}, use_global_device_ids=true | all-gather | bytes 786432 | tf_op jit(solution)/shard_map/all_gather | solution.py:81
  217.2 2.9 %collective-permute-start.20 = (bf16[256,512]{1,0:T(8,128)(2,1)}, bf16[256,512]{1,0:T(8,128)(2,1)}, u32[]{:S(2)}, u32[]{:S(2)}) collective-permute-start(bf16[256,512]{1,0:T(8,128)(2,1)} %slice_bitcast_fusion.42), channel_id=1, source_target_pairs={{0,4},{4,8},{8,12},{12,16},{16,20},{20,24},{24,28},{28,0},{1,5},{5... | collective-permute-start | bytes 786440 | tf_op jit(solution)/shard_map/ppermute | solution.py:13
  225.5 3.3 %collective-permute-start.22 = (bf16[256,512]{1,0:T(8,128)(2,1)}, bf16[256,512]{1,0:T(8,128)(2,1)}, u32[]{:S(2)}, u32[]{:S(2)}) collective-permute-start(bf16[256,512]{1,0:T(8,128)(2,1)} %slice_bitcast_fusion.42), channel_id=1, source_target_pairs={{0,12},{4,16},{8,20},{12,24},{16,28},{20,0},{24,4},{28,8},{1,13},{... | collective-permute-start | bytes 786440 | tf_op jit(solution)/shard_map/ppermute | solution.py:13
  229.9 2.5 fusion.12
  235.8 12.2 %collective-permute-done.19 = bf16[256,512]{1,0:T(8,128)(2,1)} collective-permute-done((bf16[256,512]{1,0:T(8,128)(2,1)}, bf16[256,512]{1,0:T(8,128)(2,1)}, u32[]{:S(2)}, u32[]{:S(2)}) %collective-permute-start.19) | collective-permute-done | bytes 262176 | tf_op jit(solution)/shard_map/ppermute | solution.py:13
  262.9 3.3 %fusion.11 = f32[4,128,256]{2,1,0:T(8,128)} fusion(f32[4,128,256]{2,1,0:T(8,128)} %convolution_multiply_fusion, f32[4,128,256]{2,1,0:T(8,128)} %convolution_multiply_fusion.1, f32[4,128,256]{2,1,0:T(8,128)} %convolution_multiply_fusion.2, f32[4,128,256]{2,1,0:T(8,128)} %convolution_multiply_fusion.3, f32[4,128,256]{2,1,0:T(8,128)} %convolution_multiply_fusion.4, ...), kind=kOutput, calls=%fused_computation.17 | convolution fusion | flops 68026368 | bytes 4456452 | tf_op jit(solution)/shard_map/hts,shc->thc/dot_general | solution.py:53
  269.5 7.0 %all_gather.23 = bf16[256,1024]{1,0:T(8,128)(2,1)S(1)} all-gather(bf16[256,512]{1,0:T(8,128)(2,1)S(1)} %fusion.45), channel_id=1, replica_groups=mesh['seq'=8,'chan'=2,'section'=2] {'chan'}, dimensions={1}, use_global_device_ids=true | all-gather | bytes 786432 | tf_op jit(solution)/shard_map/all_gather | solution.py:91
  (132 shorter events, 120.0 us)
Async XLA Ops:
  10.6 32.3 %copy-start.2 = (bf16[256,2,512]{2,0,1:T(8,128)(2,1)}, bf16[256,2,512]{2,0,1:T(8,128)(2,1)S(1)}, u32[]{:S(2)}) copy-start(bf16[256,2,512]{2,0,1:T(8,128)(2,1)S(1)} %fusion.4) | copy-start | bytes 1572868
  11.3 52.8 %collective-permute-start = (bf16[256,512]{1,0:T(8,128)(2,1)}, bf16[256,512]{1,0:T(8,128)(2,1)}, u32[]{:S(2)}, u32[]{:S(2)}) collective-permute-start(bf16[256,512]{1,0:T(8,128)(2,1)} %slice_bitcast_fusion.40), channel_id=1, source_target_pairs={{0,16},{4,20},{8,24},{12,28},{16,0},{20,4},{24,8},{28,12},{1,17},{... | collective-permute-start | bytes 786440 | tf_op jit(solution)/shard_map/ppermute | solution.py:13
  13.9 55.4 %collective-permute-start.5 = (bf16[256,512]{1,0:T(8,128)(2,1)}, bf16[256,512]{1,0:T(8,128)(2,1)S(1)}, u32[]{:S(2)}, u32[]{:S(2)}) collective-permute-start(bf16[256,512]{1,0:T(8,128)(2,1)} %slice_bitcast_fusion.40), channel_id=1, source_target_pairs={{0,8},{4,12},{8,16},{12,20},{16,24},{20,28},{24,0},{28,4},{1,9},{5... | collective-permute-start | bytes 786440 | tf_op jit(solution)/shard_map/ppermute | solution.py:13
  13.9 61.1 %collective-permute-start.4 = (bf16[256,512]{1,0:T(8,128)(2,1)}, bf16[256,512]{1,0:T(8,128)(2,1)}, u32[]{:S(2)}, u32[]{:S(2)}) collective-permute-start(bf16[256,512]{1,0:T(8,128)(2,1)} %slice_bitcast_fusion.40), channel_id=1, source_target_pairs={{0,4},{4,8},{8,12},{12,16},{16,20},{20,24},{24,28},{28,0},{1,5},{5... | collective-permute-start | bytes 786440 | tf_op jit(solution)/shard_map/ppermute | solution.py:13
  14.8 63.7 %collective-permute-start.3 = (bf16[256,512]{1,0:T(8,128)(2,1)}, bf16[256,512]{1,0:T(8,128)(2,1)}, u32[]{:S(2)}, u32[]{:S(2)}) collective-permute-start(bf16[256,512]{1,0:T(8,128)(2,1)} %slice_bitcast_fusion.40), channel_id=1, source_target_pairs={{0,28},{4,0},{8,4},{12,8},{16,12},{20,16},{24,20},{28,24},{1,29},{... | collective-permute-start | bytes 786440 | tf_op jit(solution)/shard_map/ppermute | solution.py:13
  15.9 66.0 %collective-permute-start.2 = (bf16[256,512]{1,0:T(8,128)(2,1)}, bf16[256,512]{1,0:T(8,128)(2,1)}, u32[]{:S(2)}, u32[]{:S(2)}) collective-permute-start(bf16[256,512]{1,0:T(8,128)(2,1)} %slice_bitcast_fusion.40), channel_id=1, source_target_pairs={{0,24},{4,28},{8,0},{12,4},{16,8},{20,12},{24,16},{28,20},{1,25},{... | collective-permute-start | bytes 786440 | tf_op jit(solution)/shard_map/ppermute | solution.py:13
  64.1 21.2 %collective-permute-start.6 = (bf16[256,512]{1,0:T(8,128)(2,1)}, bf16[256,512]{1,0:T(8,128)(2,1)}, u32[]{:S(2)}, u32[]{:S(2)}) collective-permute-start(bf16[256,512]{1,0:T(8,128)(2,1)} %slice_bitcast_fusion.40), channel_id=1, source_target_pairs={{0,12},{4,16},{8,20},{12,24},{16,28},{20,0},{24,4},{28,8},{1,13},{... | collective-permute-start | bytes 786440 | tf_op jit(solution)/shard_map/ppermute | solution.py:13
  70.0 18.8 %collective-permute-start.1 = (bf16[256,512]{1,0:T(8,128)(2,1)}, bf16[256,512]{1,0:T(8,128)(2,1)}, u32[]{:S(2)}, u32[]{:S(2)}) collective-permute-start(bf16[256,512]{1,0:T(8,128)(2,1)} %slice_bitcast_fusion.40), channel_id=1, source_target_pairs={{0,20},{4,24},{8,28},{12,0},{16,4},{20,8},{24,12},{28,16},{1,21},{... | collective-permute-start | bytes 786440 | tf_op jit(solution)/shard_map/ppermute | solution.py:13
  104.1 2.4 collective-permute-start.7
  119.1 20.5 %collective-permute-start.8 = (bf16[256,512]{1,0:T(8,128)(2,1)}, bf16[256,512]{1,0:T(8,128)(2,1)}, u32[]{:S(2)}, u32[]{:S(2)}) collective-permute-start(bf16[256,512]{1,0:T(8,128)(2,1)} %slice_bitcast_fusion.41), channel_id=1, source_target_pairs={{0,16},{4,20},{8,24},{12,28},{16,0},{20,4},{24,8},{28,12},{1,17},{... | collective-permute-start | bytes 786440 | tf_op jit(solution)/shard_map/ppermute | solution.py:13
  128.9 26.2 %collective-permute-start.10 = (bf16[256,512]{1,0:T(8,128)(2,1)}, bf16[256,512]{1,0:T(8,128)(2,1)}, u32[]{:S(2)}, u32[]{:S(2)}) collective-permute-start(bf16[256,512]{1,0:T(8,128)(2,1)} %slice_bitcast_fusion.41), channel_id=1, source_target_pairs={{0,24},{4,28},{8,0},{12,4},{16,8},{20,12},{24,16},{28,20},{1,25},{... | collective-permute-start | bytes 786440 | tf_op jit(solution)/shard_map/ppermute | solution.py:13
  130.3 35.1 %collective-permute-start.11 = (bf16[256,512]{1,0:T(8,128)(2,1)}, bf16[256,512]{1,0:T(8,128)(2,1)}, u32[]{:S(2)}, u32[]{:S(2)}) collective-permute-start(bf16[256,512]{1,0:T(8,128)(2,1)} %slice_bitcast_fusion.41), channel_id=1, source_target_pairs={{0,28},{4,0},{8,4},{12,8},{16,12},{20,16},{24,20},{28,24},{1,29},{... | collective-permute-start | bytes 786440 | tf_op jit(solution)/shard_map/ppermute | solution.py:13
  130.8 38.0 %collective-permute-start.12 = (bf16[256,512]{1,0:T(8,128)(2,1)}, bf16[256,512]{1,0:T(8,128)(2,1)}, u32[]{:S(2)}, u32[]{:S(2)}) collective-permute-start(bf16[256,512]{1,0:T(8,128)(2,1)} %slice_bitcast_fusion.41), channel_id=1, source_target_pairs={{0,4},{4,8},{8,12},{12,16},{16,20},{20,24},{24,28},{28,0},{1,5},{5... | collective-permute-start | bytes 786440 | tf_op jit(solution)/shard_map/ppermute | solution.py:13
  133.2 39.1 %collective-permute-start.13 = (bf16[256,512]{1,0:T(8,128)(2,1)}, bf16[256,512]{1,0:T(8,128)(2,1)}, u32[]{:S(2)}, u32[]{:S(2)}) collective-permute-start(bf16[256,512]{1,0:T(8,128)(2,1)} %slice_bitcast_fusion.41), channel_id=1, source_target_pairs={{0,8},{4,12},{8,16},{12,20},{16,24},{20,28},{24,0},{28,4},{1,9},{5... | collective-permute-start | bytes 786440 | tf_op jit(solution)/shard_map/ppermute | solution.py:13
  139.6 36.2 %collective-permute-start.14 = (bf16[256,512]{1,0:T(8,128)(2,1)}, bf16[256,512]{1,0:T(8,128)(2,1)}, u32[]{:S(2)}, u32[]{:S(2)}) collective-permute-start(bf16[256,512]{1,0:T(8,128)(2,1)} %slice_bitcast_fusion.41), channel_id=1, source_target_pairs={{0,12},{4,16},{8,20},{12,24},{16,28},{20,0},{24,4},{28,8},{1,13},{... | collective-permute-start | bytes 786440 | tf_op jit(solution)/shard_map/ppermute | solution.py:13
  155.1 24.1 %collective-permute-start.9 = (bf16[256,512]{1,0:T(8,128)(2,1)}, bf16[256,512]{1,0:T(8,128)(2,1)}, u32[]{:S(2)}, u32[]{:S(2)}) collective-permute-start(bf16[256,512]{1,0:T(8,128)(2,1)} %slice_bitcast_fusion.41), channel_id=1, source_target_pairs={{0,20},{4,24},{8,28},{12,0},{16,4},{20,8},{24,12},{28,16},{1,21},{... | collective-permute-start | bytes 786440 | tf_op jit(solution)/shard_map/ppermute | solution.py:13
  194.4 2.4 collective-permute-start.15
  209.4 16.1 %collective-permute-start.16 = (bf16[256,512]{1,0:T(8,128)(2,1)}, bf16[256,512]{1,0:T(8,128)(2,1)}, u32[]{:S(2)}, u32[]{:S(2)}) collective-permute-start(bf16[256,512]{1,0:T(8,128)(2,1)} %slice_bitcast_fusion.42), channel_id=1, source_target_pairs={{0,16},{4,20},{8,24},{12,28},{16,0},{20,4},{24,8},{28,12},{1,17},{... | collective-permute-start | bytes 786440 | tf_op jit(solution)/shard_map/ppermute | solution.py:13
  217.2 15.2 %collective-permute-start.18 = (bf16[256,512]{1,0:T(8,128)(2,1)}, bf16[256,512]{1,0:T(8,128)(2,1)}, u32[]{:S(2)}, u32[]{:S(2)}) collective-permute-start(bf16[256,512]{1,0:T(8,128)(2,1)} %slice_bitcast_fusion.42), channel_id=1, source_target_pairs={{0,24},{4,28},{8,0},{12,4},{16,8},{20,12},{24,16},{28,20},{1,25},{... | collective-permute-start | bytes 786440 | tf_op jit(solution)/shard_map/ppermute | solution.py:13
  217.2 30.8 %collective-permute-start.19 = (bf16[256,512]{1,0:T(8,128)(2,1)}, bf16[256,512]{1,0:T(8,128)(2,1)}, u32[]{:S(2)}, u32[]{:S(2)}) collective-permute-start(bf16[256,512]{1,0:T(8,128)(2,1)} %slice_bitcast_fusion.42), channel_id=1, source_target_pairs={{0,28},{4,0},{8,4},{12,8},{16,12},{20,16},{24,20},{28,24},{1,29},{... | collective-permute-start | bytes 786440 | tf_op jit(solution)/shard_map/ppermute | solution.py:13
  217.2 34.3 %collective-permute-start.20 = (bf16[256,512]{1,0:T(8,128)(2,1)}, bf16[256,512]{1,0:T(8,128)(2,1)}, u32[]{:S(2)}, u32[]{:S(2)}) collective-permute-start(bf16[256,512]{1,0:T(8,128)(2,1)} %slice_bitcast_fusion.42), channel_id=1, source_target_pairs={{0,4},{4,8},{8,12},{12,16},{16,20},{20,24},{24,28},{28,0},{1,5},{5... | collective-permute-start | bytes 786440 | tf_op jit(solution)/shard_map/ppermute | solution.py:13
  220.1 34.8 %collective-permute-start.21 = (bf16[256,512]{1,0:T(8,128)(2,1)}, bf16[256,512]{1,0:T(8,128)(2,1)}, u32[]{:S(2)}, u32[]{:S(2)}) collective-permute-start(bf16[256,512]{1,0:T(8,128)(2,1)} %slice_bitcast_fusion.42), channel_id=1, source_target_pairs={{0,8},{4,12},{8,16},{12,20},{16,24},{20,28},{24,0},{28,4},{1,9},{5... | collective-permute-start | bytes 786440 | tf_op jit(solution)/shard_map/ppermute | solution.py:13
  225.5 32.8 %collective-permute-start.22 = (bf16[256,512]{1,0:T(8,128)(2,1)}, bf16[256,512]{1,0:T(8,128)(2,1)}, u32[]{:S(2)}, u32[]{:S(2)}) collective-permute-start(bf16[256,512]{1,0:T(8,128)(2,1)} %slice_bitcast_fusion.42), channel_id=1, source_target_pairs={{0,12},{4,16},{8,20},{12,24},{16,28},{20,0},{24,4},{28,8},{1,13},{... | collective-permute-start | bytes 786440 | tf_op jit(solution)/shard_map/ppermute | solution.py:13
  232.4 29.4 %collective-permute-start.17 = (bf16[256,512]{1,0:T(8,128)(2,1)}, bf16[256,512]{1,0:T(8,128)(2,1)}, u32[]{:S(2)}, u32[]{:S(2)}) collective-permute-start(bf16[256,512]{1,0:T(8,128)(2,1)} %slice_bitcast_fusion.42), channel_id=1, source_target_pairs={{0,20},{4,24},{8,28},{12,0},{16,4},{20,8},{24,12},{28,16},{1,21},{... | collective-permute-start | bytes 786440 | tf_op jit(solution)/shard_map/ppermute | solution.py:13
  (7 other events, 50.2 us)
where the time goes:
time: 282 us; the launch traced here: 279 us
  local copies, waits for them, and re-layouts  76.3 us (27%)
  matrix products  62.3 us (22%)
  blocking collectives  48.3 us (17%)
  starting transfers between devices  36.6 us (13%)
  waiting for transfers between devices  27 us (10%)
  between operations  18.1 us (6%)
  other arithmetic  10.3 us (4%)
    dot_general x24, matrix products, toeplitz_apply(): jnp.einsum('hts,shc->thc', toeplitz[block_lag + reach], shaped, preferred...  58.8 us
    ppermute x21, starting transfers between devices, shifted(): lax.ppermute(value, axis, [(i, (i + by) % size) for i in range(size)])  34 us
    all_gather x3, blocking collectives, per_device(): lax.all_gather(layer_input, 'chan', axis=1, tiled=True)  27.2 us
    ppermute x21, waiting for transfers between devices, shifted(): lax.ppermute(value, axis, [(i, (i + by) % size) for i in range(size)])  24.8 us
    reshape x21, local copies, waits for them, and re-layouts, toeplitz_apply(): shaped = source.reshape(block_len, local_heads, head_width)  22.7 us
    all_gather x3, blocking collectives, per_device(): lax.all_gather(gated, 'chan', axis=1, tiled=True)  21.1 us
    reshape x1, local copies, waits for them, and re-layouts, toeplitz_stack(): tiled[..., :BLK * (2 * BLK - 1)]  19.5 us
    unnamed x26, local copies, waits for them, and re-layouts  8.37 us
  transfers between devices with their start and end apart: 23, of which 6 were waited for; matrix products, arithmetic and copies ran while one was open for 40% of the time, Pallas kernels for 0%

commit v1 on v0

--- a/solution.py
+++ b/solution.py
@@ -6,6 +6,18 @@
 BLK = 256
 BAND = 8
 MB = 2
+
+
+def gather_by_bits(x, axis, dim):
+    ways, here, lap = (lax.axis_size(axis), lax.axis_index(axis), x.shape[dim])
+    line, have = (x, 1)
+    while have < ways:
+        line = jnp.concatenate(
+            [line, lax.ppermute(line, axis, [(d, (d - have) % ways) for d in range(ways)])],
+            axis=dim,
+        )
+        have = 2 * have
+    return jnp.roll(line, here * lap, axis=dim)
 
 
 def shifted(value, axis, by):
@@ -88,9 +100,7 @@
         mixed = convolve(signal, toeplitz, widths, micro_batch)
         gated = (jax.nn.silu(gating.astype(jnp.float32)) * mixed).astype(jnp.bfloat16)
         result = jnp.dot(
-            lax.all_gather(gated, "chan", axis=1, tiled=True),
-            output_weight,
-            preferred_element_type=jnp.float32,
+            gather_by_bits(gated, "chan", 1), output_weight, preferred_element_type=jnp.float32
         ).astype(jnp.bfloat16)
         slot_mask = jnp.arange(MB) == step_index - section_index
         record = jnp.where(slot_mask[None, :, None, None], result[None, None], record)

time: 282 us -> 273 us (0.968)
  the two profiles are of different devices: /device:TPU:14 before, /device:TPU:0 now
where the time goes in v1:
time: 273 us; the launch traced here: 270 us
  starting transfers between devices  69.9 us (26%)
  local copies, waits for them, and re-layouts  63.5 us (23%)
  matrix products  58.4 us (21%)
  blocking collectives  28.4 us (10%)
  waiting for transfers between devices  21.9 us (8%)
  between operations  18.3 us (7%)
  other arithmetic  9.82 us (4%)
    ppermute x21, starting transfers between devices, shifted(): lax.ppermute(value, axis, [(i, (i + by) % size) for i in range(size)])  62.6 us
    dot_general x24, matrix products, toeplitz_apply(): jnp.einsum('hts,shc->thc', toeplitz[block_lag + reach], shaped, preferred...  51.1 us
    all_gather x3, blocking collectives, per_device(): lax.all_gather(layer_input, 'chan', axis=1, tiled=True)  28.4 us
    reshape x21, local copies, waits for them, and re-layouts, toeplitz_apply(): shaped = source.reshape(block_len, local_heads, head_width)  19.9 us
    reshape x1, local copies, waits for them, and re-layouts, toeplitz_stack(): tiled[..., :BLK * (2 * BLK - 1)]  19.5 us
    ppermute x3, waiting for transfers between devices, gather_by_bits(): lax.ppermute(line, axis, [(d, (d - have) % ways) for d in range(ways)])  16.1 us
    slice x1, local copies, waits for them, and re-layouts, toeplitz_stack(): tiled[..., :BLK * (2 * BLK - 1)]  7.13 us
    unnamed x22, local copies, waits for them, and re-layouts  5.96 us
  transfers between devices with their start and end apart: 26, of which 7 were waited for; matrix products, arithmetic and copies ran while one was open for 36% of the time, Pallas kernels for 0%

profile of v1, /device:TPU:0, one launch (start us, length us, event | category | flops | bytes accessed | tf_op | source)
XLA Modules:
  0.0 270.3 jit_solution(17440151759809433869)
XLA Ops:
  1.1 9.9 %all-gather = bf16[1,256,1024]{2,1,0:T(8,128)(2,1)S(1)} all-gather(bf16[1,256,512]{2,1,0:T(8,128)(2,1)S(1)} %slice_select_fusion), channel_id=2, replica_groups=mesh['seq'=8,'chan'=2,'section'=2] {'chan'}, dimensions={2}, use_global_device_ids=true | all-gather | bytes 786432 | tf_op jit(solution)/shard_map/all_gather | solution.py:93
  12.6 2.8 %collective-permute-start = (bf16[256,512]{1,0:T(8,128)(2,1)}, bf16[256,512]{1,0:T(8,128)(2,1)}, u32[]{:S(2)}, u32[]{:S(2)}) collective-permute-start(bf16[256,512]{1,0:T(8,128)(2,1)} %slice_bitcast_fusion.40), channel_id=1, source_target_pairs={{0,16},{4,20},{8,24},{12,28},{16,0},{20,4},{24,8},{28,12},{1,17},{... | collective-permute-start | bytes 786440 | tf_op jit(solution)/shard_map/ppermute | solution.py:25
  18.5 3.2 %collective-permute-start.3 = (bf16[256,512]{1,0:T(8,128)(2,1)}, bf16[256,512]{1,0:T(8,128)(2,1)}, u32[]{:S(2)}, u32[]{:S(2)}) collective-permute-start(bf16[256,512]{1,0:T(8,128)(2,1)} %slice_bitcast_fusion.40), channel_id=1, source_target_pairs={{0,28},{4,0},{8,4},{12,8},{16,12},{20,16},{24,20},{28,24},{1,29},{... | collective-permute-start | bytes 786440 | tf_op jit(solution)/shard_map/ppermute | solution.py:25
  36.1 3.8 %tile.4 = bf16[8,4,256,512]{3,0,2,1:T(8,128)(2,1)} broadcast(bf16[8,4,512]{2,0,1:T(8,128)(2,1)S(1)} %pad.4.clone), dimensions={0,1,3} | broadcast | bytes 8421376 | tf_op jit(solution)/shard_map/tile | solution.py:48
  40.0 7.1 %slice.139 = bf16[8,4,130816]{2,0,1:T(8,128)(2,1)} slice(bf16[8,4,131072]{2,0,1:T(8,128)(2,1)} %bitcast.195), slice={[0:8], [0:4], [0:130816]} | slice | bytes 16744448 | tf_op jit(solution)/shard_map/slice | solution.py:49
  47.1 19.5 %reshape.214 = bf16[8,4,256,511]{3,2,0,1:T(8,128)(2,1)} reshape(bf16[8,4,130816]{2,0,1:T(8,128)(2,1)} %slice.139) | data formatting | bytes 16744448 | tf_op jit(solution)/shard_map/reshape | solution.py:49
  69.5 2.4 fusion.26
  71.9 3.8 %collective-permute-start.1 = (bf16[256,512]{1,0:T(8,128)(2,1)}, bf16[256,512]{1,0:T(8,128)(2,1)}, u32[]{:S(2)}, u32[]{:S(2)}) collective-permute-start(bf16[256,512]{1,0:T(8,128)(2,1)} %slice_bitcast_fusion.40), channel_id=1, source_target_pairs={{0,20},{4,24},{8,28},{12,0},{16,4},{20,8},{24,12},{28,16},{1,21},{... | collective-permute-start | bytes 786440 | tf_op jit(solution)/shard_map/ppermute | solution.py:25
  91.5 3.0 %fusion.25 = f32[4,128,256]{2,1,0:T(8,128)} fusion(f32[4,128,256]{2,1,0:T(8,128)} %convolution_multiply_fusion.16, f32[4,128,256]{2,1,0:T(8,128)S(1)} %convolution_multiply_fusion.17, f32[4,128,256]{2,1,0:T(8,128)S(1)} %convolution_multiply_fusion.18, f32[4,128,256]{2,1,0:T(8,128)} %convolution_multiply_fusion.19, ...), kind=kOutput, calls=%fused_computation.47 | convolution fusion | flops 68026368 | bytes 4456452 | tf_op jit(solution)/shard_map/hts,shc->thc/dot_general | solution.py:65
  98.4 4.9 %collective-permute-done.7 = bf16[256,512]{1,0:T(8,128)(2,1)S(1)} collective-permute-done((bf16[256,512]{1,0:T(8,128)(2,1)S(1)}, bf16[256,512]{1,0:T(8,128)(2,1)S(1)}, u32[]{:S(2)}, u32[]{:S(2)}) %collective-permute-start.7) | collective-permute-done | bytes 262176 | tf_op jit(solution)/shard_map/ppermute | solution.py:16
  108.5 9.2 %all_gather.10 = bf16[256,1024]{1,0:T(8,128)(2,1)S(1)} all-gather(bf16[256,512]{1,0:T(8,128)(2,1)S(1)} %bitcast_select_fusion.1), channel_id=1, replica_groups=mesh['seq'=8,'chan'=2,'section'=2] {'chan'}, dimensions={1}, use_global_device_ids=true | all-gather | bytes 786432 | tf_op jit(solution)/shard_map/all_gather | solution.py:93
  125.4 4.0 %collective-permute-start.11 = (bf16[256,512]{1,0:T(8,128)(2,1)}, bf16[256,512]{1,0:T(8,128)(2,1)}, u32[]{:S(2)}, u32[]{:S(2)}) collective-permute-start(bf16[256,512]{1,0:T(8,128)(2,1)} %slice_bitcast_fusion.41), channel_id=1, source_target_pairs={{0,24},{4,28},{8,0},{12,4},{16,8},{20,12},{24,16},{28,20},{1,25},{... | collective-permute-start | bytes 786440 | tf_op jit(solution)/shard_map/ppermute | solution.py:25
  134.8 4.0 %collective-permute-start.15 = (bf16[256,512]{1,0:T(8,128)(2,1)}, bf16[256,512]{1,0:T(8,128)(2,1)}, u32[]{:S(2)}, u32[]{:S(2)}) collective-permute-start(bf16[256,512]{1,0:T(8,128)(2,1)} %slice_bitcast_fusion.41), channel_id=1, source_target_pairs={{0,12},{4,16},{8,20},{12,24},{16,28},{20,0},{24,4},{28,8},{1,13},{... | collective-permute-start | bytes 786440 | tf_op jit(solution)/shard_map/ppermute | solution.py:25
  141.3 13.7 %collective-permute-start.10 = (bf16[256,512]{1,0:T(8,128)(2,1)}, bf16[256,512]{1,0:T(8,128)(2,1)}, u32[]{:S(2)}, u32[]{:S(2)}) collective-permute-start(bf16[256,512]{1,0:T(8,128)(2,1)} %slice_bitcast_fusion.41), channel_id=1, source_target_pairs={{0,20},{4,24},{8,28},{12,0},{16,4},{20,8},{24,12},{28,16},{1,21},{... | collective-permute-start | bytes 786440 | tf_op jit(solution)/shard_map/ppermute | solution.py:25
  164.9 2.4 convolution_multiply_fusion.9
  171.8 3.0 %fusion.18 = f32[4,128,256]{2,1,0:T(8,128)} fusion(f32[4,128,256]{2,1,0:T(8,128)} %convolution_multiply_fusion.8, f32[4,128,256]{2,1,0:T(8,128)} %convolution_multiply_fusion.9, f32[4,128,256]{2,1,0:T(8,128)} %convolution_multiply_fusion.10, f32[4,128,256]{2,1,0:T(8,128)S(1)} %convolution_multiply_fusion.11, ...), kind=kOutput, calls=%fused_computation.32 | convolution fusion | flops 68026368 | bytes 4456452 | tf_op jit(solution)/shard_map/hts,shc->thc/dot_general | solution.py:65
  178.7 6.4 %collective-permute-done.16 = bf16[256,512]{1,0:T(8,128)(2,1)S(1)} collective-permute-done((bf16[256,512]{1,0:T(8,128)(2,1)S(1)}, bf16[256,512]{1,0:T(8,128)(2,1)S(1)}, u32[]{:S(2)}, u32[]{:S(2)}) %collective-permute-start.16) | collective-permute-done | bytes 262176 | tf_op jit(solution)/shard_map/ppermute | solution.py:16
  190.2 9.2 %all_gather.11 = bf16[256,1024]{1,0:T(8,128)(2,1)S(1)} all-gather(bf16[256,512]{1,0:T(8,128)(2,1)S(1)} %bitcast_select_fusion), channel_id=1, replica_groups=mesh['seq'=8,'chan'=2,'section'=2] {'chan'}, dimensions={1}, use_global_device_ids=true | all-gather | bytes 786432 | tf_op jit(solution)/shard_map/all_gather | solution.py:93
  206.7 3.4 %collective-permute-start.20 = (bf16[256,512]{1,0:T(8,128)(2,1)}, bf16[256,512]{1,0:T(8,128)(2,1)}, u32[]{:S(2)}, u32[]{:S(2)}) collective-permute-start(bf16[256,512]{1,0:T(8,128)(2,1)} %slice_bitcast_fusion.42), channel_id=1, source_target_pairs={{0,24},{4,28},{8,0},{12,4},{16,8},{20,12},{24,16},{28,20},{1,25},{... | collective-permute-start | bytes 786440 | tf_op jit(solution)/shard_map/ppermute | solution.py:25
  216.3 3.2 %collective-permute-start.24 = (bf16[256,512]{1,0:T(8,128)(2,1)}, bf16[256,512]{1,0:T(8,128)(2,1)}, u32[]{:S(2)}, u32[]{:S(2)}) collective-permute-start(bf16[256,512]{1,0:T(8,128)(2,1)} %slice_bitcast_fusion.42), channel_id=1, source_target_pairs={{0,12},{4,16},{8,20},{12,24},{16,28},{20,0},{24,4},{28,8},{1,13},{... | collective-permute-start | bytes 786440 | tf_op jit(solution)/shard_map/ppermute | solution.py:25
  222.0 16.1 %collective-permute-start.19 = (bf16[256,512]{1,0:T(8,128)(2,1)}, bf16[256,512]{1,0:T(8,128)(2,1)}, u32[]{:S(2)}, u32[]{:S(2)}) collective-permute-start(bf16[256,512]{1,0:T(8,128)(2,1)} %slice_bitcast_fusion.42), channel_id=1, source_target_pairs={{0,20},{4,24},{8,28},{12,0},{16,4},{20,8},{24,12},{28,16},{1,21},{... | collective-permute-start | bytes 786440 | tf_op jit(solution)/shard_map/ppermute | solution.py:25
  247.9 2.4 convolution_multiply_fusion.1
  254.8 3.0 %fusion.11 = f32[4,128,256]{2,1,0:T(8,128)} fusion(f32[4,128,256]{2,1,0:T(8,128)} %convolution_multiply_fusion, f32[4,128,256]{2,1,0:T(8,128)} %convolution_multiply_fusion.1, f32[4,128,256]{2,1,0:T(8,128)} %convolution_multiply_fusion.2, f32[4,128,256]{2,1,0:T(8,128)S(1)} %convolution_multiply_fusion.3, f32[4,128,256]{2,1,0:T(8,128)S(1)} %convolution_multiply_fusion.4, ...), kind=kOutput, calls=%fused_computation.17 | convolution fusion | flops 68026368 | bytes 4456452 | tf_op jit(solution)/shard_map/hts,shc->thc/dot_general | solution.py:65
  261.7 4.9 %collective-permute-done.25 = bf16[256,512]{1,0:T(8,128)(2,1)S(1)} collective-permute-done((bf16[256,512]{1,0:T(8,128)(2,1)S(1)}, bf16[256,512]{1,0:T(8,128)(2,1)S(1)}, u32[]{:S(2)}, u32[]{:S(2)}) %collective-permute-start.25) | collective-permute-done | bytes 262176 | tf_op jit(solution)/shard_map/ppermute | solution.py:16
  (131 shorter events, 106.5 us)
Async XLA Ops:
  12.6 55.8 %collective-permute-start = (bf16[256,512]{1,0:T(8,128)(2,1)}, bf16[256,512]{1,0:T(8,128)(2,1)}, u32[]{:S(2)}, u32[]{:S(2)}) collective-permute-start(bf16[256,512]{1,0:T(8,128)(2,1)} %slice_bitcast_fusion.40), channel_id=1, source_target_pairs={{0,16},{4,20},{8,24},{12,28},{16,0},{20,4},{24,8},{28,12},{1,17},{... | collective-permute-start | bytes 786440 | tf_op jit(solution)/shard_map/ppermute | solution.py:25
  15.4 56.6 %collective-permute-start.5 = (bf16[256,512]{1,0:T(8,128)(2,1)}, bf16[256,512]{1,0:T(8,128)(2,1)S(1)}, u32[]{:S(2)}, u32[]{:S(2)}) collective-permute-start(bf16[256,512]{1,0:T(8,128)(2,1)} %slice_bitcast_fusion.40), channel_id=1, source_target_pairs={{0,8},{4,12},{8,16},{12,20},{16,24},{20,28},{24,0},{28,4},{1,9},{5... | collective-permute-start | bytes 786440 | tf_op jit(solution)/shard_map/ppermute | solution.py:25
  17.0 60.5 %collective-permute-start.4 = (bf16[256,512]{1,0:T(8,128)(2,1)}, bf16[256,512]{1,0:T(8,128)(2,1)}, u32[]{:S(2)}, u32[]{:S(2)}) collective-permute-start(bf16[256,512]{1,0:T(8,128)(2,1)} %slice_bitcast_fusion.40), channel_id=1, source_target_pairs={{0,4},{4,8},{8,12},{12,16},{16,20},{20,24},{24,28},{28,0},{1,5},{5... | collective-permute-start | bytes 786440 | tf_op jit(solution)/shard_map/ppermute | solution.py:25
  18.5 61.6 %collective-permute-start.3 = (bf16[256,512]{1,0:T(8,128)(2,1)}, bf16[256,512]{1,0:T(8,128)(2,1)}, u32[]{:S(2)}, u32[]{:S(2)}) collective-permute-start(bf16[256,512]{1,0:T(8,128)(2,1)} %slice_bitcast_fusion.40), channel_id=1, source_target_pairs={{0,28},{4,0},{8,4},{12,8},{16,12},{20,16},{24,20},{28,24},{1,29},{... | collective-permute-start | bytes 786440 | tf_op jit(solution)/shard_map/ppermute | solution.py:25
  21.7 61.8 %collective-permute-start.2 = (bf16[256,512]{1,0:T(8,128)(2,1)}, bf16[256,512]{1,0:T(8,128)(2,1)}, u32[]{:S(2)}, u32[]{:S(2)}) collective-permute-start(bf16[256,512]{1,0:T(8,128)(2,1)} %slice_bitcast_fusion.40), channel_id=1, source_target_pairs={{0,24},{4,28},{8,0},{12,4},{16,8},{20,12},{24,16},{28,20},{1,25},{... | collective-permute-start | bytes 786440 | tf_op jit(solution)/shard_map/ppermute | solution.py:25
  68.4 18.6 %collective-permute-start.6 = (bf16[256,512]{1,0:T(8,128)(2,1)}, bf16[256,512]{1,0:T(8,128)(2,1)}, u32[]{:S(2)}, u32[]{:S(2)}) collective-permute-start(bf16[256,512]{1,0:T(8,128)(2,1)} %slice_bitcast_fusion.40), channel_id=1, source_target_pairs={{0,12},{4,16},{8,20},{12,24},{16,28},{20,0},{24,4},{28,8},{1,13},{... | collective-permute-start | bytes 786440 | tf_op jit(solution)/shard_map/ppermute | solution.py:25
  71.9 18.5 %collective-permute-start.1 = (bf16[256,512]{1,0:T(8,128)(2,1)}, bf16[256,512]{1,0:T(8,128)(2,1)}, u32[]{:S(2)}, u32[]{:S(2)}) collective-permute-start(bf16[256,512]{1,0:T(8,128)(2,1)} %slice_bitcast_fusion.40), channel_id=1, source_target_pairs={{0,20},{4,24},{8,28},{12,0},{16,4},{20,8},{24,12},{28,16},{1,21},{... | collective-permute-start | bytes 786440 | tf_op jit(solution)/shard_map/ppermute | solution.py:25
  96.8 6.4 %collective-permute-start.7 = (bf16[256,512]{1,0:T(8,128)(2,1)S(1)}, bf16[256,512]{1,0:T(8,128)(2,1)S(1)}, u32[]{:S(2)}, u32[]{:S(2)}) collective-permute-start(bf16[256,512]{1,0:T(8,128)(2,1)S(1)} %fusion.62), channel_id=1, source_target_pairs={{0,2},{2,0},{1,3},{3,1},{4,6},{6,4},{5,7},{7,5},{8,10},{10,8},{9,1... | collective-permute-start | bytes 786440 | tf_op jit(solution)/shard_map/ppermute | solution.py:16
  119.2 15.6 %collective-permute-start.9 = (bf16[256,512]{1,0:T(8,128)(2,1)}, bf16[256,512]{1,0:T(8,128)(2,1)S(1)}, u32[]{:S(2)}, u32[]{:S(2)}) collective-permute-start(bf16[256,512]{1,0:T(8,128)(2,1)} %slice_bitcast_fusion.41), channel_id=1, source_target_pairs={{0,16},{4,20},{8,24},{12,28},{16,0},{20,4},{24,8},{28,12},{1,17},{... | collective-permute-start | bytes 786440 | tf_op jit(solution)/shard_map/ppermute | solution.py:25
  125.4 16.0 %collective-permute-start.11 = (bf16[256,512]{1,0:T(8,128)(2,1)}, bf16[256,512]{1,0:T(8,128)(2,1)}, u32[]{:S(2)}, u32[]{:S(2)}) collective-permute-start(bf16[256,512]{1,0:T(8,128)(2,1)} %slice_bitcast_fusion.41), channel_id=1, source_target_pairs={{0,24},{4,28},{8,0},{12,4},{16,8},{20,12},{24,16},{28,20},{1,25},{... | collective-permute-start | bytes 786440 | tf_op jit(solution)/shard_map/ppermute | solution.py:25
  129.3 28.4 %collective-permute-start.12 = (bf16[256,512]{1,0:T(8,128)(2,1)}, bf16[256,512]{1,0:T(8,128)(2,1)}, u32[]{:S(2)}, u32[]{:S(2)}) collective-permute-start(bf16[256,512]{1,0:T(8,128)(2,1)} %slice_bitcast_fusion.41), channel_id=1, source_target_pairs={{0,28},{4,0},{8,4},{12,8},{16,12},{20,16},{24,20},{28,24},{1,29},{... | collective-permute-start | bytes 786440 | tf_op jit(solution)/shard_map/ppermute | solution.py:25
  130.7 29.6 %collective-permute-start.13 = (bf16[256,512]{1,0:T(8,128)(2,1)}, bf16[256,512]{1,0:T(8,128)(2,1)}, u32[]{:S(2)}, u32[]{:S(2)}) collective-permute-start(bf16[256,512]{1,0:T(8,128)(2,1)} %slice_bitcast_fusion.41), channel_id=1, source_target_pairs={{0,4},{4,8},{8,12},{12,16},{16,20},{20,24},{24,28},{28,0},{1,5},{5... | collective-permute-start | bytes 786440 | tf_op jit(solution)/shard_map/ppermute | solution.py:25
  131.4 32.4 %collective-permute-start.14 = (bf16[256,512]{1,0:T(8,128)(2,1)}, bf16[256,512]{1,0:T(8,128)(2,1)}, u32[]{:S(2)}, u32[]{:S(2)}) collective-permute-start(bf16[256,512]{1,0:T(8,128)(2,1)} %slice_bitcast_fusion.41), channel_id=1, source_target_pairs={{0,8},{4,12},{8,16},{12,20},{16,24},{20,28},{24,0},{28,4},{1,9},{5... | collective-permute-start | bytes 786440 | tf_op jit(solution)/shard_map/ppermute | solution.py:25
  134.8 32.4 %collective-permute-start.15 = (bf16[256,512]{1,0:T(8,128)(2,1)}, bf16[256,512]{1,0:T(8,128)(2,1)}, u32[]{:S(2)}, u32[]{:S(2)}) collective-permute-start(bf16[256,512]{1,0:T(8,128)(2,1)} %slice_bitcast_fusion.41), channel_id=1, source_target_pairs={{0,12},{4,16},{8,20},{12,24},{16,28},{20,0},{24,4},{28,8},{1,13},{... | collective-permute-start | bytes 786440 | tf_op jit(solution)/shard_map/ppermute | solution.py:25
  141.3 29.3 %collective-permute-start.10 = (bf16[256,512]{1,0:T(8,128)(2,1)}, bf16[256,512]{1,0:T(8,128)(2,1)}, u32[]{:S(2)}, u32[]{:S(2)}) collective-permute-start(bf16[256,512]{1,0:T(8,128)(2,1)} %slice_bitcast_fusion.41), channel_id=1, source_target_pairs={{0,20},{4,24},{8,28},{12,0},{16,4},{20,8},{24,12},{28,16},{1,21},{... | collective-permute-start | bytes 786440 | tf_op jit(solution)/shard_map/ppermute | solution.py:25
  177.1 7.9 %collective-permute-start.16 = (bf16[256,512]{1,0:T(8,128)(2,1)S(1)}, bf16[256,512]{1,0:T(8,128)(2,1)S(1)}, u32[]{:S(2)}, u32[]{:S(2)}) collective-permute-start(bf16[256,512]{1,0:T(8,128)(2,1)S(1)} %fusion.61), channel_id=1, source_target_pairs={{0,2},{2,0},{1,3},{3,1},{4,6},{6,4},{5,7},{7,5},{8,10},{10,8},{9,1... | collective-permute-start | bytes 786440 | tf_op jit(solution)/shard_map/ppermute | solution.py:16
  201.0 15.3 %collective-permute-start.18 = (bf16[256,512]{1,0:T(8,128)(2,1)}, bf16[256,512]{1,0:T(8,128)(2,1)S(1)}, u32[]{:S(2)}, u32[]{:S(2)}) collective-permute-start(bf16[256,512]{1,0:T(8,128)(2,1)} %slice_bitcast_fusion.42), channel_id=1, source_target_pairs={{0,16},{4,20},{8,24},{12,28},{16,0},{20,4},{24,8},{28,12},{1,17},{... | collective-permute-start | bytes 786440 | tf_op jit(solution)/shard_map/ppermute | solution.py:25
  206.7 15.3 %collective-permute-start.20 = (bf16[256,512]{1,0:T(8,128)(2,1)}, bf16[256,512]{1,0:T(8,128)(2,1)}, u32[]{:S(2)}, u32[]{:S(2)}) collective-permute-start(bf16[256,512]{1,0:T(8,128)(2,1)} %slice_bitcast_fusion.42), channel_id=1, source_target_pairs={{0,24},{4,28},{8,0},{12,4},{16,8},{20,12},{24,16},{28,20},{1,25},{... | collective-permute-start | bytes 786440 | tf_op jit(solution)/shard_map/ppermute | solution.py:25
  210.1 30.6 %collective-permute-start.21 = (bf16[256,512]{1,0:T(8,128)(2,1)}, bf16[256,512]{1,0:T(8,128)(2,1)}, u32[]{:S(2)}, u32[]{:S(2)}) collective-permute-start(bf16[256,512]{1,0:T(8,128)(2,1)} %slice_bitcast_fusion.42), channel_id=1, source_target_pairs={{0,28},{4,0},{8,4},{12,8},{16,12},{20,16},{24,20},{28,24},{1,29},{... | collective-permute-start | bytes 786440 | tf_op jit(solution)/shard_map/ppermute | solution.py:25
  210.5 32.9 %collective-permute-start.22 = (bf16[256,512]{1,0:T(8,128)(2,1)}, bf16[256,512]{1,0:T(8,128)(2,1)}, u32[]{:S(2)}, u32[]{:S(2)}) collective-permute-start(bf16[256,512]{1,0:T(8,128)(2,1)} %slice_bitcast_fusion.42), channel_id=1, source_target_pairs={{0,4},{4,8},{8,12},{12,16},{16,20},{20,24},{24,28},{28,0},{1,5},{5... | collective-permute-start | bytes 786440 | tf_op jit(solution)/shard_map/ppermute | solution.py:25
  212.2 34.7 %collective-permute-start.23 = (bf16[256,512]{1,0:T(8,128)(2,1)}, bf16[256,512]{1,0:T(8,128)(2,1)}, u32[]{:S(2)}, u32[]{:S(2)}) collective-permute-start(bf16[256,512]{1,0:T(8,128)(2,1)} %slice_bitcast_fusion.42), channel_id=1, source_target_pairs={{0,8},{4,12},{8,16},{12,20},{16,24},{20,28},{24,0},{28,4},{1,9},{5... | collective-permute-start | bytes 786440 | tf_op jit(solution)/shard_map/ppermute | solution.py:25
  216.3 34.0 %collective-permute-start.24 = (bf16[256,512]{1,0:T(8,128)(2,1)}, bf16[256,512]{1,0:T(8,128)(2,1)}, u32[]{:S(2)}, u32[]{:S(2)}) collective-permute-start(bf16[256,512]{1,0:T(8,128)(2,1)} %slice_bitcast_fusion.42), channel_id=1, source_target_pairs={{0,12},{4,16},{8,20},{12,24},{16,28},{20,0},{24,4},{28,8},{1,13},{... | collective-permute-start | bytes 786440 | tf_op jit(solution)/shard_map/ppermute | solution.py:25
  222.0 31.7 %collective-permute-start.19 = (bf16[256,512]{1,0:T(8,128)(2,1)}, bf16[256,512]{1,0:T(8,128)(2,1)}, u32[]{:S(2)}, u32[]{:S(2)}) collective-permute-start(bf16[256,512]{1,0:T(8,128)(2,1)} %slice_bitcast_fusion.42), channel_id=1, source_target_pairs={{0,20},{4,24},{8,28},{12,0},{16,4},{20,8},{24,12},{28,16},{1,21},{... | collective-permute-start | bytes 786440 | tf_op jit(solution)/shard_map/ppermute | solution.py:25
  260.1 6.4 %collective-permute-start.25 = (bf16[256,512]{1,0:T(8,128)(2,1)S(1)}, bf16[256,512]{1,0:T(8,128)(2,1)S(1)}, u32[]{:S(2)}, u32[]{:S(2)}) collective-permute-start(bf16[256,512]{1,0:T(8,128)(2,1)S(1)} %fusion.60), channel_id=1, source_target_pairs={{0,2},{2,0},{1,3},{3,1},{4,6},{6,4},{5,7},{7,5},{8,10},{10,8},{9,1... | collective-permute-start | bytes 786440 | tf_op jit(solution)/shard_map/ppermute | solution.py:16
  (8 other events, 84.0 us)
